TPU v7x, 512 devices: a whole 4x8x8 slice. The times are simulated.
512 devices in a mesh: ctx: 128 (over y, z, core), head: 4 (over x).
Axes of the slice: x: 4, y: 8, z: 8, core: 2. Of those that a mesh axis runs over, the one named last changes fastest.
Arguments:
- tokens: bfloat16 [2, 16384, 4096], P(None, 'ctx', 'head'), may hold values from -6 to 6
- w_query: bfloat16 [4096, 2048], P('ctx', 'head'), may hold values from -0.09375 to 0.09375
- w_key: bfloat16 [4096, 2048], P('ctx', 'head'), may hold values from -0.09375 to 0.09375
- w_value: bfloat16 [4096, 2048], P('ctx', 'head'), may hold values from -0.09375 to 0.09375
- norm_gain: float32 [2048], P('head'), may hold values from 0.1 to 1.9
Outputs:
- attended: bfloat16 [2, 16384, 2048], P(None, 'ctx', 'head')
All inputs are finite; a program needn't handle non-finite values.
Results may differ from a plain program's by a relative error of at most 0.0072.
Values may be sent and summed in bfloat16 or wider, within the bound.
No kernel may reach another device: no remote copies, remote signals or barrier semaphores. Data moves between devices by JAX's collectives and lax.ppermute only.
A program may use at most 192 MiB of HBM per device.

v0:
```python
import jax
import jax.numpy as jnp
from jax import lax
from jax.sharding import PartitionSpec as P

HD = 128


def entering(part, axis, combine, identity):
    place = lax.axis_index(axis)
    gathered = lax.all_gather(part, axis)
    state = jnp.zeros_like(part) + jnp.asarray(identity, part.dtype)

    def one(hop, state):
        return combine(state, lax.dynamic_index_in_dim(gathered, hop, 0, False))

    return lax.fori_loop(0, place, one, state)


def add_states(earlier, later):
    return earlier + later


def body(tokens, w_query, w_key, w_value, norm_gain):
    gathered = lax.all_gather(tokens, "head", axis=2, tiled=True)
    seq_count, span_len, model_dim = gathered.shape
    token_rows = gathered.reshape(seq_count * span_len, model_dim)
    features = w_query.shape[1]
    query_full = lax.all_gather(w_query, "ctx", axis=0, tiled=True)
    query_sum = jnp.dot(token_rows, query_full, preferred_element_type=jnp.float32)
    key_full = lax.all_gather(w_key, "ctx", axis=0, tiled=True)
    key_sum = jnp.dot(token_rows, key_full, preferred_element_type=jnp.float32)
    value_full = lax.all_gather(w_value, "ctx", axis=0, tiled=True)
    value_sum = jnp.dot(token_rows, value_full, preferred_element_type=jnp.float32)
    head_count = features // HD

    def heads_first(projected):
        shaped = projected.astype(jnp.bfloat16).reshape(seq_count, span_len, head_count, HD)
        return shaped.transpose(0, 2, 1, 3)

    query = heads_first(jax.nn.silu(query_sum))
    key_all = heads_first(jax.nn.silu(key_sum))
    value_all = heads_first(value_sum)
    positions = jnp.arange(span_len)
    causal = positions[:, None] >= positions[None, :]
    scores = jnp.einsum("shtd,shud->shtu", query, key_all, preferred_element_type=jnp.float32)
    masked = jnp.where(causal, scores, 0.0).astype(jnp.bfloat16)
    local_out = jnp.einsum("shtu,shud->shtd", masked, value_all, preferred_element_type=jnp.float32)
    states = jnp.einsum("shud,shue->shde", key_all, value_all, preferred_element_type=jnp.float32)
    prefix = entering(states, "ctx", add_states, jnp.zeros_like(states))
    from_prefix = jnp.einsum(
        "shtd,shde->shte", query, prefix.astype(jnp.bfloat16), preferred_element_type=jnp.float32
    )
    total = local_out + from_prefix
    scale_inv = lax.rsqrt(jnp.mean(total * total, axis=-1, keepdims=True) + 1e-06)
    gain_view = norm_gain.reshape(1, head_count, 1, HD)
    normed = total * scale_inv * gain_view
    return normed.transpose(0, 2, 1, 3).reshape(seq_count, span_len, features).astype(jnp.bfloat16)


def solution(mesh):
    in_specs = (
        P(None, "ctx", "head"),
        P("ctx", "head"),
        P("ctx", "head"),
        P("ctx", "head"),
        P("head"),
    )
    out_specs = P(None, "ctx", "head")
    return jax.shard_map(body, mesh=mesh, in_specs=in_specs, out_specs=out_specs, check_vma=False)
```

profile of v0, /device:TPU:505, one launch (start us, length us, event | category | flops | bytes accessed | tf_op | source)
XLA Modules:
  0.0 681.2 jit_solution(4002791682843718653)
XLA Ops:
  9.4 35.0 %all-gather.7.cloned.1.call-done = bf16[2,128,4096]{2,1,0:T(8,128)(2,1)} async-done(((bf16[2,128,1024]{2,1,0:T(8,128)(2,1)}), bf16[2,128,4096]{2,1,0:T(8,128)(2,1)}) %all-gather.7.cloned.1.call-update) | async-done | bytes 2097168 | tf_op jit(solution)/shard_map/all_gather | solution.py:25
  44.3 84.9 %all-gather.11.cloned.1.call-done = bf16[4096,512]{1,0:T(8,128)(2,1)} async-done(((bf16[32,512]{1,0:T(8,128)(2,1)}), bf16[4096,512]{1,0:T(8,128)(2,1)}) %all-gather.11.cloned.1.call-update) | async-done | bytes 4194320 | tf_op jit(solution)/shard_map/all_gather | solution.py:31
  129.2 4.3 multiply_convert_fusion
  133.8 79.8 %all-gather.13.cloned.1.call-done = bf16[4096,512]{1,0:T(8,128)(2,1)} async-done(((bf16[32,512]{1,0:T(8,128)(2,1)}), bf16[4096,512]{1,0:T(8,128)(2,1)}) %all-gather.13.cloned.1.call-update) | async-done | bytes 4194320 | tf_op jit(solution)/shard_map/all_gather | solution.py:33
  213.6 3.4 convolution_convert_fusion
  218.2 79.6 %all-gather.9.cloned.1.call-done = bf16[4096,512]{1,0:T(8,128)(2,1)} async-done(((bf16[32,512]{1,0:T(8,128)(2,1)}), bf16[4096,512]{1,0:T(8,128)(2,1)}) %all-gather.9.cloned.1.call-update) | async-done | bytes 4194320 | tf_op jit(solution)/shard_map/all_gather | solution.py:29
  297.8 3.5 multiply_convert_fusion.1
  301.9 219.8 %all-gather.15.cloned.1.call-done = f32[256,4,128,128]{3,2,1,0:T(8,128)} async-done(((f32[2,4,128,128]{3,2,1,0:T(8,128)}), f32[256,4,128,128]{3,2,1,0:T(8,128)}) %all-gather.15.cloned.1.call-update) | async-done | bytes 67108880 | tf_op jit(solution)/shard_map/all_gather | solution.py:11
  521.7 151.5 %while.10 = (s32[]{:T(128)}, f32[2,4,128,128]{3,2,1,0:T(8,128)S(1)}, s32[]{:T(128)}, f32[128,2,4,128,128]{4,3,2,1,0:T(8,128)}, s32[]{:T(128)}, /*index=5*/s32[]{:T(128)}, s32[]{:T(128)}) while((s32[]{:T(128)}, f32[2,4,128,128]{3,2,1,0:T(8,128)S(1)}, s32[]{:T(128)}, f32[128,2,4,128,128]{4,3,2,1,0:T(8,128)}, s32[]{:T(128)}, ...), condition=%wide.region_1.2_spmd, body=%wide.region_0.1_spmd.sunk | while | flops 131077 | bytes 1572987 | solution.py:17
  525.3 1.2 bitcast_add_fusion.2
  526.5 1.2 bitcast_add_fusion.2
  527.7 1.2 bitcast_add_fusion.2
  528.9 1.2 bitcast_add_fusion.2
  530.1 1.2 bitcast_add_fusion.2
  531.3 1.2 bitcast_add_fusion.2
  536.1 1.2 bitcast_add_fusion.2
  537.3 1.2 bitcast_add_fusion.2
  538.4 1.2 bitcast_add_fusion.2
  539.6 1.2 bitcast_add_fusion.2
  540.8 1.2 bitcast_add_fusion.2
  542.0 1.2 bitcast_add_fusion.2
  548.0 1.2 bitcast_add_fusion.2
  549.2 1.2 bitcast_add_fusion.2
  550.4 1.2 bitcast_add_fusion.2
  551.6 1.2 bitcast_add_fusion.2
  552.8 1.2 bitcast_add_fusion.2
  554.0 1.2 bitcast_add_fusion.2
  558.7 1.2 bitcast_add_fusion.2
  559.9 1.2 bitcast_add_fusion.2
  561.1 1.2 bitcast_add_fusion.2
  562.3 1.2 bitcast_add_fusion.2
  563.5 1.2 bitcast_add_fusion.2
  (130 shorter events, 127.8 us)
Async XLA Ops:
  6.5 37.8 %all-gather.7.cloned.1.call-start = ((), (), s32[]{:S(2)}) async-start(), calls=%async_computation | async-start | bytes 2621440 | tf_op jit(solution)/shard_map/all_gather | solution.py:25
  7.3 122.0 %all-gather.11.cloned.1.call-start = ((), (), s32[]{:S(2)}) async-start(), calls=%async_computation.2 | async-start | bytes 4227072 | tf_op jit(solution)/shard_map/all_gather | solution.py:31
  8.0 205.6 %all-gather.13.cloned.1.call-start = ((), (), s32[]{:S(2)}) async-start(), calls=%async_computation.3 | async-start | bytes 4227072 | tf_op jit(solution)/shard_map/all_gather | solution.py:33
  8.7 289.1 %all-gather.9.cloned.1.call-start = ((), (), s32[]{:S(2)}) async-start(), calls=%async_computation.1 | async-start | bytes 4227072 | tf_op jit(solution)/shard_map/all_gather | solution.py:29
  9.3 512.4 %all-gather.15.cloned.1.call-start = ((), (), s32[]{:S(2)}) async-start(), calls=%async_computation.4 | async-start | bytes 67633152 | tf_op jit(solution)/shard_map/all_gather | solution.py:11
  129.2 84.4 %copy-start.1 = (bf16[2,128,4096]{2,1,0:T(8,128)(2,1)S(1)}, bf16[2,128,4096]{2,1,0:T(8,128)(2,1)}, u32[]{:S(2)}) copy-start(bf16[2,128,4096]{2,1,0:T(8,128)(2,1)} %all-gather.7.cloned.1.call-done) | copy-start | bytes 6291460
  521.7 151.9 %copy-start = (f32[512]{0:T(512)S(1)}, f32[512]{0:T(512)}, u32[]{:S(2)}) copy-start(f32[512]{0:T(512)} %param.11) | copy-start | bytes 6148
Sparse Core Ops, SparseCore 0:
  9.4 34.8 all-gather.6
  47.5 81.7 all-gather.10
  132.4 81.1 all-gather.12
  216.6 81.1 all-gather.8
  300.8 220.8 all-gather.14
where the time goes:
time: 687 us; the launch traced here: 681 us
  waiting for transfers between devices  502 us (73%)
  other arithmetic  149 us (22%)
  between operations  13.2 us (2%)
  matrix products  13.1 us (2%)
    all_gather x1, waiting for transfers between devices, entering(): gathered = lax.all_gather(part, axis)  220 us
    add x127, other arithmetic, add_states(): return earlier + later  149 us
    all_gather x1, waiting for transfers between devices, body(): key_full = lax.all_gather(w_key, 'ctx', axis=0, tiled=True)  84.9 us
    all_gather x1, waiting for transfers between devices, body(): value_full = lax.all_gather(w_value, 'ctx', axis=0, tiled=True)  79.8 us
    all_gather x1, waiting for transfers between devices, body(): query_full = lax.all_gather(w_query, 'ctx', axis=0, tiled=True)  79.6 us
    all_gather x1, waiting for transfers between devices, body(): gathered = lax.all_gather(tokens, 'head', axis=2, tiled=True)  35 us
  transfers between devices with their start and end apart: 5, of which 5 were waited for; matrix products, arithmetic and copies ran while one was open for 2% of the time, Pallas kernels for 0%

commit v1 on v0

--- a/solution.py
+++ b/solution.py
@@ -22,7 +22,8 @@
 
 
 def body(tokens, w_query, w_key, w_value, norm_gain):
-    gathered = lax.all_gather(tokens, "head", axis=2, tiled=True)
+    out_arr = jnp.stack([tokens] * lax.axis_size("head"))
+    gathered = jnp.concatenate(lax.all_to_all(out_arr, "head", 0, 0), axis=2)
     seq_count, span_len, model_dim = gathered.shape
     token_rows = gathered.reshape(seq_count * span_len, model_dim)
     features = w_query.shape[1]

time: 687 us -> 649 us (0.945)
  waiting for transfers between devices: 502 us -> 431 us
  blocking collectives: 0 us -> 29.3 us
    all_gather x1 -> x0, waiting for transfers between devices: 35 us -> none  [body(): gathered = lax.all_gather(tokens, 'head', axis=2, tiled=True)]
    all_gather x1, waiting for transfers between devices: 79.8 us -> 49 us  [body(): value_full = lax.all_gather(w_value, 'ctx', axis=0, tiled=True)]
    all_to_all x0 -> x1, blocking collectives: none -> 29.3 us  [body(): gathered = jnp.concatenate(lax.all_to_all(out_arr, 'head', 0, 0), axis=2)]
  transfers between devices with their start and end apart: 5 -> 4, of which waited for: 5 -> 4; matrix products, arithmetic and copies ran while one was open for 2% -> 3% of each run, Pallas kernels for 0% -> 0%
where the time goes in v1:
time: 649 us; the launch traced here: 643 us
  waiting for transfers between devices  431 us (66%)
  other arithmetic  149 us (23%)
  blocking collectives  29.3 us (5%)
  between operations  13.2 us (2%)
  matrix products  12.3 us (2%)
    all_gather x1, waiting for transfers between devices, entering(): gathered = lax.all_gather(part, axis)  220 us
    add x127, other arithmetic, add_states(): return earlier + later  149 us
    all_gather x1, waiting for transfers between devices, body(): key_full = lax.all_gather(w_key, 'ctx', axis=0, tiled=True)  80.9 us
    all_gather x1, waiting for transfers between devices, body(): query_full = lax.all_gather(w_query, 'ctx', axis=0, tiled=True)  79.5 us
    all_gather x1, waiting for transfers between devices, body(): value_full = lax.all_gather(w_value, 'ctx', axis=0, tiled=True)  49 us
    all_to_all x1, blocking collectives, body(): gathered = jnp.concatenate(lax.all_to_all(out_arr, 'head', 0, 0), axis=2)  29.3 us
  transfers between devices with their start and end apart: 4, of which 4 were waited for; matrix products, arithmetic and copies ran while one was open for 3% of the time, Pallas kernels for 0%

profile of v1, /device:TPU:505, one launch (start us, length us, event | category | flops | bytes accessed | tf_op | source)
XLA Modules:
  0.0 643.0 jit_solution(12263145506521153286)
XLA Ops:
  8.8 1.3 stack.2
  10.1 29.3 %all_to_all.5 = bf16[4,2,128,1024]{3,2,1,0:T(8,128)(2,1)S(1)} all-to-all(bf16[4,2,128,1024]{3,2,1,0:T(8,128)(2,1)S(1)} %stack.2), channel_id=1, replica_groups=mesh['ctx'=128,'head'=4] {'head'}, dimensions={0} | all-to-all | bytes 4194304 | tf_op jit(solution)/shard_map/all_to_all | solution.py:26
  39.4 1.6 copy.18
  41.9 49.0 %all-gather.10.cloned.1.call-done = bf16[4096,512]{1,0:T(8,128)(2,1)} async-done(((bf16[32,512]{1,0:T(8,128)(2,1)}), bf16[4096,512]{1,0:T(8,128)(2,1)}) %all-gather.10.cloned.1.call-update) | async-done | bytes 4194320 | tf_op jit(solution)/shard_map/all_gather | solution.py:34
  90.9 3.4 convolution_convert_fusion
  94.4 80.9 %all-gather.8.cloned.1.call-done = bf16[4096,512]{1,0:T(8,128)(2,1)} async-done(((bf16[32,512]{1,0:T(8,128)(2,1)}), bf16[4096,512]{1,0:T(8,128)(2,1)}) %all-gather.8.cloned.1.call-update) | async-done | bytes 4194320 | tf_op jit(solution)/shard_map/all_gather | solution.py:32
  175.3 3.5 multiply_convert_fusion
  180.2 79.5 %all-gather.6.cloned.1.call-done = bf16[4096,512]{1,0:T(8,128)(2,1)} async-done(((bf16[32,512]{1,0:T(8,128)(2,1)}), bf16[4096,512]{1,0:T(8,128)(2,1)}) %all-gather.6.cloned.1.call-update) | async-done | bytes 4194320 | tf_op jit(solution)/shard_map/all_gather | solution.py:30
  259.7 3.5 multiply_convert_fusion.1
  263.7 219.8 %all-gather.12.cloned.1.call-done = f32[256,4,128,128]{3,2,1,0:T(8,128)} async-done(((f32[2,4,128,128]{3,2,1,0:T(8,128)}), f32[256,4,128,128]{3,2,1,0:T(8,128)}) %all-gather.12.cloned.1.call-update) | async-done | bytes 67108880 | tf_op jit(solution)/shard_map/all_gather | solution.py:11
  483.6 151.5 %while.10 = (s32[]{:T(128)}, f32[2,4,128,128]{3,2,1,0:T(8,128)S(1)}, s32[]{:T(128)}, f32[128,2,4,128,128]{4,3,2,1,0:T(8,128)}, s32[]{:T(128)}, /*index=5*/s32[]{:T(128)}, s32[]{:T(128)}) while((s32[]{:T(128)}, f32[2,4,128,128]{3,2,1,0:T(8,128)S(1)}, s32[]{:T(128)}, f32[128,2,4,128,128]{4,3,2,1,0:T(8,128)}, s32[]{:T(128)}, ...), condition=%wide.region_1.2_spmd, body=%wide.region_0.1_spmd.sunk | while | flops 131077 | bytes 1572987 | solution.py:17
  483.6 1.2 bitcast_add_fusion.2
  484.8 1.2 bitcast_add_fusion.2
  486.0 1.2 bitcast_add_fusion.2
  487.2 1.2 bitcast_add_fusion.2
  491.9 1.2 bitcast_add_fusion.2
  493.1 1.2 bitcast_add_fusion.2
  494.3 1.2 bitcast_add_fusion.2
  495.5 1.2 bitcast_add_fusion.2
  496.7 1.2 bitcast_add_fusion.2
  497.9 1.2 bitcast_add_fusion.2
  503.9 1.2 bitcast_add_fusion.2
  505.1 1.2 bitcast_add_fusion.2
  506.3 1.2 bitcast_add_fusion.2
  507.5 1.2 bitcast_add_fusion.2
  508.6 1.2 bitcast_add_fusion.2
  509.8 1.2 bitcast_add_fusion.2
  514.6 1.2 bitcast_add_fusion.2
  515.8 1.2 bitcast_add_fusion.2
  517.0 1.2 bitcast_add_fusion.2
  518.2 1.2 bitcast_add_fusion.2
  519.4 1.2 bitcast_add_fusion.2
  (129 shorter events, 130.5 us)
Async XLA Ops:
  6.5 84.4 %all-gather.10.cloned.1.call-start = ((), (), s32[]{:S(2)}) async-start(), calls=%async_computation.3 | async-start | bytes 4227072 | tf_op jit(solution)/shard_map/all_gather | solution.py:34
  7.3 168.0 %all-gather.8.cloned.1.call-start = ((), (), s32[]{:S(2)}) async-start(), calls=%async_computation.2 | async-start | bytes 4227072 | tf_op jit(solution)/shard_map/all_gather | solution.py:32
  8.0 251.7 %all-gather.6.cloned.1.call-start = ((), (), s32[]{:S(2)}) async-start(), calls=%async_computation.1 | async-start | bytes 4227072 | tf_op jit(solution)/shard_map/all_gather | solution.py:30
  8.7 474.8 %all-gather.12.cloned.1.call-start = ((), (), s32[]{:S(2)}) async-start(), calls=%async_computation.4 | async-start | bytes 67633152 | tf_op jit(solution)/shard_map/all_gather | solution.py:11
  483.6 151.9 %copy-start = (f32[512]{0:T(512)S(1)}, f32[512]{0:T(512)}, u32[]{:S(2)}) copy-start(f32[512]{0:T(512)} %param.11) | copy-start | bytes 6148
Sparse Core Ops, SparseCore 0:
  10.5 80.4 all-gather.9
  94.1 81.1 all-gather.7
  178.4 81.1 all-gather.5
  262.6 220.8 all-gather.11
